TPU v7x, 256 devices: a whole 4x4x8 slice. The times are simulated.
256 devices in a mesh: bench: 32 (over x, y, core), sweep: 8 (over z).
Axes of the slice: x: 4, y: 4, z: 8, core: 2. Of those that a mesh axis runs over, the one named last changes fastest.
Arguments:
- finished: bfloat16 [1024, 8, 64, 128], P('bench', 'sweep'), may hold values from -6 to 6
- noise: bfloat16 [1024, 8, 64, 128], P('bench', 'sweep'), may hold values from -6 to 6
- factors: bfloat16 [1024, 8, 8, 128, 128], P('bench', 'sweep'), may hold values from -0.1875 to 0.1875
- chol: bfloat16 [1024, 8, 128, 128], P('bench', 'sweep'), may hold values from -0.1875 to 0.1875
- front_w: bfloat16 [1024, 8, 128, 128], P('bench', 'sweep'), may hold values from -0.5 to 0.5
- parents: int32 [1024, 8, 8], P('bench', 'sweep'), may hold values from 0 to 1023, as said below
Outputs:
- evolved: float32 [1024, 8, 64, 128], P('bench', 'sweep')
Inputs may be any that keep to these rules, and one draw needn't show every extreme that they name: A parent row p lies on the bench owner p // 32. The 256 parents of the tiles of one bench group and sweep column name at most 16 rows of one owner, exactly 16 for some owner, and lie on at most 17 owners.
All inputs are finite; a program needn't handle non-finite values.
Results may differ from a plain program's by a relative error of at most 0.0003.
Values may be sent and summed in bfloat16 or wider, within the bound.
No kernel may reach another device: no remote copies, remote signals or barrier semaphores. Data moves between devices by JAX's collectives and lax.ppermute only.
A program may use at most 128 MiB of HBM per device.

v0:
```python
import jax
import jax.numpy as jnp
from jax import lax
from jax.sharding import PartitionSpec as P


def from_behind(array, axis, by):
    size = lax.axis_size(axis)
    pairs = [(i, i + by) for i in range(size) if 0 <= i + by < size]
    return lax.ppermute(array, axis, pairs)


def body(finished, noise, factors, chol, front_w, parents):
    pool_local = finished[:, 0]
    tile_count = noise.shape[0]
    fan = parents.shape[2]
    wanted = parents[:, 0].reshape(-1)
    whole_pool = lax.all_gather(finished, "bench", axis=0, tiled=True)
    chosen = jnp.take(whole_pool[:, 0], wanted, axis=0)
    chosen = chosen.reshape((tile_count, fan) + pool_local.shape[1:])
    local = jnp.einsum("jkrm,jkmn->jrn", chosen, factors[:, 0], preferred_element_type=jnp.float32)
    local = local + jnp.einsum(
        "jrm,jmn->jrn", noise[:, 0], chol[:, 0], preferred_element_type=jnp.float32
    )
    weights = front_w[:, 0].astype(jnp.float32)
    last_weight = weights[tile_count - 1]
    last_local = local[tile_count - 1]
    incoming = jnp.zeros_like(last_local)
    outgoing = last_local
    for step in range(lax.axis_size("sweep") - 1):
        incoming = from_behind(outgoing, "sweep", 1)
        outgoing = last_local + jnp.dot(incoming, last_weight, precision=lax.Precision.HIGHEST)
    tiles = local + jnp.einsum("rm,jmn->jrn", incoming, weights, precision=lax.Precision.HIGHEST)
    return tiles[:, None]


def solution(mesh):
    return jax.shard_map(
        body,
        mesh=mesh,
        in_specs=(
            P("bench", "sweep", None, None),
            P("bench", "sweep", None, None),
            P("bench", "sweep", None, None, None),
            P("bench", "sweep", None, None),
            P("bench", "sweep", None, None),
            P("bench", "sweep", None),
        ),
        out_specs=P("bench", "sweep", None, None),
        check_vma=False,
    )
```

profile of v0, /device:TPU:128, one launch (start us, length us, event | category | flops | bytes accessed | tf_op | source)
XLA Modules:
  0.0 163.4 jit_solution(4601643470623711922)
XLA Ops:
  6.5 0.0 copy-start
  6.5 0.0 all-gather.2.cloned.1.call-start
  6.5 0.7 all-gather.2.cloned.1.call-update
  7.3 0.8 copy.13
  8.0 0.1 reshape_squeeze.6
  8.1 0.7 compare_and_fusion
  8.8 0.1 copy.12
  8.9 80.1 %all-gather.2.cloned.1.call-done = bf16[1024,1,64,128]{3,2,1,0:T(8,128)(2,1)} async-done(((bf16[32,1,64,128]{3,2,1,0:T(8,128)(2,1)}), bf16[1024,1,64,128]{3,2,1,0:T(8,128)(2,1)}) %all-gather.2.cloned.1.call-update) | async-done | bytes 16777232 | tf_op jit(solution)/shard_map/all_gather | solution.py:18
  89.0 8.8 %gather_fusion = bf16[256,64,128]{2,1,0:T(8,128)(2,1)} fusion(bf16[1024,64,128]{2,1,0:T(8,128)(2,1)} %bitcast.73, s32[1024]{0:T(1024)S(1)} %pad_clamp_fusion), kind=kCustom, calls=%fused_computation | custom fusion | bytes 8389632 | tf_op jit(solution)/shard_map/jit(_take)/gather | solution.py:19
  97.8 0.0 copy-start.2
  97.8 0.0 copy-start.1
  97.8 6.6 %fusion.7 = f32[32,64,128]{2,1,0:T(8,128)S(1)} fusion(bf16[32,1,8,128,128]{4,3,2,1,0:T(8,128)(2,1)} %param.8, bf16[32,8,64,128]{3,2,1,0:T(8,128)(2,1)} %bitcast.72, pred[32,8]{1,0:T(8,128)(4,1)S(1)} %copy.12), kind=kOutput, calls=%fused_computation.10 | convolution fusion | flops 538968064 | bytes 13631744 | tf_op jit(solution)/shard_map/jkrm,jkmn->jrn/dot_general | solution.py:21
  104.4 0.0 copy-done
  104.4 0.0 copy-done.2
  104.4 0.4 convolution_add_fusion
  104.9 2.6 %collective-permute-start = (f32[64,128]{1,0:T(8,128)S(1)}, f32[64,128]{1,0:T(8,128)S(1)}, u32[]{:S(2)}, u32[]{:S(2)}) collective-permute-start(f32[64,128]{1,0:T(8,128)S(1)} %slice_bitcast_fusion), channel_id=1, source_target_pairs={{0,1},{1,2},{2,3},{3,4},{4,5},{5,6},{6,7},{8,9},{9,10},{10,11},{11... | collective-permute-start | bytes 98312 | tf_op jit(solution)/shard_map/ppermute | solution.py:10
  107.5 4.4 %collective-permute-done = f32[64,128]{1,0:T(8,128)S(1)} collective-permute-done((f32[64,128]{1,0:T(8,128)S(1)}, f32[64,128]{1,0:T(8,128)S(1)}, u32[]{:S(2)}, u32[]{:S(2)}) %collective-permute-start) | collective-permute-done | bytes 32800 | tf_op jit(solution)/shard_map/ppermute | solution.py:10
  111.9 0.0 copy-done.1
  111.9 0.2 convolution_add_fusion.6
  112.1 1.9 %collective-permute-start.1 = (f32[64,128]{1,0:T(8,128)S(1)}, f32[64,128]{1,0:T(8,128)S(1)}, u32[]{:S(2)}, u32[]{:S(2)}) collective-permute-start(f32[64,128]{1,0:T(8,128)S(1)} %convolution_add_fusion.6), channel_id=1, source_target_pairs={{0,1},{1,2},{2,3},{3,4},{4,5},{5,6},{6,7},{8,9},{9,10},{10,11},{11... | collective-permute-start | bytes 98312 | tf_op jit(solution)/shard_map/ppermute | solution.py:10
  114.0 5.1 %collective-permute-done.1 = f32[64,128]{1,0:T(8,128)S(1)} collective-permute-done((f32[64,128]{1,0:T(8,128)S(1)}, f32[64,128]{1,0:T(8,128)S(1)}, u32[]{:S(2)}, u32[]{:S(2)}) %collective-permute-start.1) | collective-permute-done | bytes 32800 | tf_op jit(solution)/shard_map/ppermute | solution.py:10
  119.1 0.2 convolution_add_fusion.5
  119.3 1.9 %collective-permute-start.2 = (f32[64,128]{1,0:T(8,128)S(1)}, f32[64,128]{1,0:T(8,128)S(1)}, u32[]{:S(2)}, u32[]{:S(2)}) collective-permute-start(f32[64,128]{1,0:T(8,128)S(1)} %convolution_add_fusion.5), channel_id=1, source_target_pairs={{0,1},{1,2},{2,3},{3,4},{4,5},{5,6},{6,7},{8,9},{9,10},{10,11},{11... | collective-permute-start | bytes 98312 | tf_op jit(solution)/shard_map/ppermute | solution.py:10
  121.2 5.1 %collective-permute-done.2 = f32[64,128]{1,0:T(8,128)S(1)} collective-permute-done((f32[64,128]{1,0:T(8,128)S(1)}, f32[64,128]{1,0:T(8,128)S(1)}, u32[]{:S(2)}, u32[]{:S(2)}) %collective-permute-start.2) | collective-permute-done | bytes 32800 | tf_op jit(solution)/shard_map/ppermute | solution.py:10
  126.3 0.2 convolution_add_fusion.4
  126.5 1.9 %collective-permute-start.3 = (f32[64,128]{1,0:T(8,128)S(1)}, f32[64,128]{1,0:T(8,128)S(1)}, u32[]{:S(2)}, u32[]{:S(2)}) collective-permute-start(f32[64,128]{1,0:T(8,128)S(1)} %convolution_add_fusion.4), channel_id=1, source_target_pairs={{0,1},{1,2},{2,3},{3,4},{4,5},{5,6},{6,7},{8,9},{9,10},{10,11},{11... | collective-permute-start | bytes 98312 | tf_op jit(solution)/shard_map/ppermute | solution.py:10
  128.4 5.1 %collective-permute-done.3 = f32[64,128]{1,0:T(8,128)S(1)} collective-permute-done((f32[64,128]{1,0:T(8,128)S(1)}, f32[64,128]{1,0:T(8,128)S(1)}, u32[]{:S(2)}, u32[]{:S(2)}) %collective-permute-start.3) | collective-permute-done | bytes 32800 | tf_op jit(solution)/shard_map/ppermute | solution.py:10
  133.5 0.2 convolution_add_fusion.3
  133.6 1.9 %collective-permute-start.4 = (f32[64,128]{1,0:T(8,128)S(1)}, f32[64,128]{1,0:T(8,128)S(1)}, u32[]{:S(2)}, u32[]{:S(2)}) collective-permute-start(f32[64,128]{1,0:T(8,128)S(1)} %convolution_add_fusion.3), channel_id=1, source_target_pairs={{0,1},{1,2},{2,3},{3,4},{4,5},{5,6},{6,7},{8,9},{9,10},{10,11},{11... | collective-permute-start | bytes 98312 | tf_op jit(solution)/shard_map/ppermute | solution.py:10
  135.6 5.1 %collective-permute-done.4 = f32[64,128]{1,0:T(8,128)S(1)} collective-permute-done((f32[64,128]{1,0:T(8,128)S(1)}, f32[64,128]{1,0:T(8,128)S(1)}, u32[]{:S(2)}, u32[]{:S(2)}) %collective-permute-start.4) | collective-permute-done | bytes 32800 | tf_op jit(solution)/shard_map/ppermute | solution.py:10
  140.7 0.2 convolution_add_fusion.2
  140.8 1.9 %collective-permute-start.5 = (f32[64,128]{1,0:T(8,128)S(1)}, f32[64,128]{1,0:T(8,128)S(1)}, u32[]{:S(2)}, u32[]{:S(2)}) collective-permute-start(f32[64,128]{1,0:T(8,128)S(1)} %convolution_add_fusion.2), channel_id=1, source_target_pairs={{0,1},{1,2},{2,3},{3,4},{4,5},{5,6},{6,7},{8,9},{9,10},{10,11},{11... | collective-permute-start | bytes 98312 | tf_op jit(solution)/shard_map/ppermute | solution.py:10
  142.8 5.1 %collective-permute-done.5 = f32[64,128]{1,0:T(8,128)S(1)} collective-permute-done((f32[64,128]{1,0:T(8,128)S(1)}, f32[64,128]{1,0:T(8,128)S(1)}, u32[]{:S(2)}, u32[]{:S(2)}) %collective-permute-start.5) | collective-permute-done | bytes 32800 | tf_op jit(solution)/shard_map/ppermute | solution.py:10
  147.9 0.2 convolution_add_fusion.1
  148.0 1.9 %collective-permute-start.6 = (f32[64,128]{1,0:T(8,128)S(1)}, f32[64,128]{1,0:T(8,128)S(1)}, u32[]{:S(2)}, u32[]{:S(2)}) collective-permute-start(f32[64,128]{1,0:T(8,128)S(1)} %convolution_add_fusion.1), channel_id=1, source_target_pairs={{0,1},{1,2},{2,3},{3,4},{4,5},{5,6},{6,7},{8,9},{9,10},{10,11},{11... | collective-permute-start | bytes 98312 | tf_op jit(solution)/shard_map/ppermute | solution.py:10
  150.0 5.1 %collective-permute-done.6 = f32[64,128]{1,0:T(8,128)S(1)} collective-permute-done((f32[64,128]{1,0:T(8,128)S(1)}, f32[64,128]{1,0:T(8,128)S(1)}, u32[]{:S(2)}, u32[]{:S(2)}) %collective-permute-start.6) | collective-permute-done | bytes 32800 | tf_op jit(solution)/shard_map/ppermute | solution.py:10
  155.0 1.5 fusion.6
  (3 shorter events, 0.0 us)
Async XLA Ops:
  6.5 97.9 %copy-start = (bf16[32,1,128,128]{3,2,1,0:T(8,128)(2,1)S(1)}, bf16[32,1,128,128]{3,2,1,0:T(8,128)(2,1)}, u32[]{:S(2)}) copy-start(bf16[32,1,128,128]{3,2,1,0:T(8,128)(2,1)} %param.9) | copy-start | bytes 3145732
  6.5 82.4 %all-gather.2.cloned.1.call-start = ((), (), s32[]{:S(2)}) async-start(), calls=%async_computation | async-start | bytes 17301504 | tf_op jit(solution)/shard_map/all_gather | solution.py:18
  97.8 6.6 %copy-start.2 = (bf16[32,1,64,128]{3,2,1,0:T(8,128)(2,1)S(1)}, bf16[32,1,64,128]{3,2,1,0:T(8,128)(2,1)}, u32[]{:S(2)}) copy-start(bf16[32,1,64,128]{3,2,1,0:T(8,128)(2,1)} %param.7) | copy-start | bytes 1572868
  97.8 14.1 %copy-start.1 = (bf16[32,1,128,128]{3,2,1,0:T(8,128)(2,1)S(1)}, bf16[32,1,128,128]{3,2,1,0:T(8,128)(2,1)}, u32[]{:S(2)}) copy-start(bf16[32,1,128,128]{3,2,1,0:T(8,128)(2,1)} %param.10) | copy-start | bytes 3145732
  104.9 7.0 %collective-permute-start = (f32[64,128]{1,0:T(8,128)S(1)}, f32[64,128]{1,0:T(8,128)S(1)}, u32[]{:S(2)}, u32[]{:S(2)}) collective-permute-start(f32[64,128]{1,0:T(8,128)S(1)} %slice_bitcast_fusion), channel_id=1, source_target_pairs={{0,1},{1,2},{2,3},{3,4},{4,5},{5,6},{6,7},{8,9},{9,10},{10,11},{11... | collective-permute-start | bytes 98312 | tf_op jit(solution)/shard_map/ppermute | solution.py:10
  112.1 7.0 %collective-permute-start.1 = (f32[64,128]{1,0:T(8,128)S(1)}, f32[64,128]{1,0:T(8,128)S(1)}, u32[]{:S(2)}, u32[]{:S(2)}) collective-permute-start(f32[64,128]{1,0:T(8,128)S(1)} %convolution_add_fusion.6), channel_id=1, source_target_pairs={{0,1},{1,2},{2,3},{3,4},{4,5},{5,6},{6,7},{8,9},{9,10},{10,11},{11... | collective-permute-start | bytes 98312 | tf_op jit(solution)/shard_map/ppermute | solution.py:10
  119.3 7.0 %collective-permute-start.2 = (f32[64,128]{1,0:T(8,128)S(1)}, f32[64,128]{1,0:T(8,128)S(1)}, u32[]{:S(2)}, u32[]{:S(2)}) collective-permute-start(f32[64,128]{1,0:T(8,128)S(1)} %convolution_add_fusion.5), channel_id=1, source_target_pairs={{0,1},{1,2},{2,3},{3,4},{4,5},{5,6},{6,7},{8,9},{9,10},{10,11},{11... | collective-permute-start | bytes 98312 | tf_op jit(solution)/shard_map/ppermute | solution.py:10
  126.5 7.0 %collective-permute-start.3 = (f32[64,128]{1,0:T(8,128)S(1)}, f32[64,128]{1,0:T(8,128)S(1)}, u32[]{:S(2)}, u32[]{:S(2)}) collective-permute-start(f32[64,128]{1,0:T(8,128)S(1)} %convolution_add_fusion.4), channel_id=1, source_target_pairs={{0,1},{1,2},{2,3},{3,4},{4,5},{5,6},{6,7},{8,9},{9,10},{10,11},{11... | collective-permute-start | bytes 98312 | tf_op jit(solution)/shard_map/ppermute | solution.py:10
  133.6 7.0 %collective-permute-start.4 = (f32[64,128]{1,0:T(8,128)S(1)}, f32[64,128]{1,0:T(8,128)S(1)}, u32[]{:S(2)}, u32[]{:S(2)}) collective-permute-start(f32[64,128]{1,0:T(8,128)S(1)} %convolution_add_fusion.3), channel_id=1, source_target_pairs={{0,1},{1,2},{2,3},{3,4},{4,5},{5,6},{6,7},{8,9},{9,10},{10,11},{11... | collective-permute-start | bytes 98312 | tf_op jit(solution)/shard_map/ppermute | solution.py:10
  140.8 7.0 %collective-permute-start.5 = (f32[64,128]{1,0:T(8,128)S(1)}, f32[64,128]{1,0:T(8,128)S(1)}, u32[]{:S(2)}, u32[]{:S(2)}) collective-permute-start(f32[64,128]{1,0:T(8,128)S(1)} %convolution_add_fusion.2), channel_id=1, source_target_pairs={{0,1},{1,2},{2,3},{3,4},{4,5},{5,6},{6,7},{8,9},{9,10},{10,11},{11... | collective-permute-start | bytes 98312 | tf_op jit(solution)/shard_map/ppermute | solution.py:10
  148.0 7.0 %collective-permute-start.6 = (f32[64,128]{1,0:T(8,128)S(1)}, f32[64,128]{1,0:T(8,128)S(1)}, u32[]{:S(2)}, u32[]{:S(2)}) collective-permute-start(f32[64,128]{1,0:T(8,128)S(1)} %convolution_add_fusion.1), channel_id=1, source_target_pairs={{0,1},{1,2},{2,3},{3,4},{4,5},{5,6},{6,7},{8,9},{9,10},{10,11},{11... | collective-permute-start | bytes 98312 | tf_op jit(solution)/shard_map/ppermute | solution.py:10
Sparse Core Ops, SparseCore 0:
  9.9 79.0 all-gather.1
where the time goes:
time: 164 us; the launch traced here: 163 us
  waiting for transfers between devices  116 us (71%)
  starting transfers between devices  14.1 us (9%)
  between operations  13.5 us (8%)
  local copies, waits for them, and re-layouts  9.77 us (6%)
  matrix products  9.56 us (6%)
    all_gather x1, waiting for transfers between devices, body(): whole_pool = lax.all_gather(finished, 'bench', axis=0, tiled=True)  80.1 us
    ppermute x7, waiting for transfers between devices, from_behind(): return lax.ppermute(array, axis, pairs)  35 us
    ppermute x7, starting transfers between devices, from_behind(): return lax.ppermute(array, axis, pairs)  14.1 us
    gather x1, local copies, waits for them, and re-layouts, body(): chosen = jnp.take(whole_pool[:, 0], wanted, axis=0)  8.8 us
    dot_general x1, matrix products, body(): jnp.einsum('jkrm,jkmn->jrn', chosen, factors[:, 0], preferred_element_typ...  6.61 us
  transfers between devices with their start and end apart: 8, of which 8 were waited for; matrix products, arithmetic and copies ran while one was open for 1% of the time, Pallas kernels for 0%

commit v1 on v0

--- a/solution.py
+++ b/solution.py
@@ -15,7 +15,9 @@
     tile_count = noise.shape[0]
     fan = parents.shape[2]
     wanted = parents[:, 0].reshape(-1)
-    whole_pool = lax.all_gather(finished, "bench", axis=0, tiled=True)
+    whole_pool = jnp.concatenate(
+        lax.all_to_all(jnp.stack([finished] * lax.axis_size("bench")), "bench", 0, 0), axis=0
+    )
     chosen = jnp.take(whole_pool[:, 0], wanted, axis=0)
     chosen = chosen.reshape((tile_count, fan) + pool_local.shape[1:])
     local = jnp.einsum("jkrm,jkmn->jrn", chosen, factors[:, 0], preferred_element_type=jnp.float32)

time: 164 us -> 352 us (2.15)
  the two profiles are of different devices: /device:TPU:128 before, /device:TPU:140 now
where the time goes in v1:
time: 352 us
  waiting for transfers between devices  304 us (86%)
  starting transfers between devices  22.1 us (6%)
  local copies, waits for them, and re-layouts  16.2 us (5%)
  matrix products  9.56 us (3%)
    all_to_all x1, waiting for transfers between devices, body(): lax.all_to_all(jnp.stack([finished] * lax.axis_size('bench')), 'bench', 0...  269 us
    ppermute x7, waiting for transfers between devices, from_behind(): return lax.ppermute(array, axis, pairs)  35 us
    ppermute x7, starting transfers between devices, from_behind(): return lax.ppermute(array, axis, pairs)  14.4 us
    gather x1, local copies, waits for them, and re-layouts, body(): chosen = jnp.take(whole_pool[:, 0], wanted, axis=0)  8.8 us
    all_to_all x1, starting transfers between devices, body(): lax.all_to_all(jnp.stack([finished] * lax.axis_size('bench')), 'bench', 0...  7.67 us
    another operation x1, local copies, waits for them, and re-layouts, body(): jnp.stack([finished] * lax.axis_size('bench'))  7.14 us
  transfers between devices with their start and end apart: 8, of which 8 were waited for; matrix products, arithmetic and copies ran while one was open for 0% of the time, Pallas kernels for 0%

profile of v1, /device:TPU:140, one launch (start us, length us, event | category | flops | bytes accessed | tf_op | source)
XLA Modules:
  0.0 351.8 jit_solution(536660489840830058)
XLA Ops:
  0.0 0.0 copy-start
  0.0 7.1 %stack.2 = bf16[32,32,1,64,128]{4,3,2,1,0:T(8,128)(2,1)} broadcast(bf16[32,64,128]{2,1,0:T(8,128)(2,1)} %bitcast.74), dimensions={1,3,4} | broadcast | bytes 17301504 | tf_op jit(solution)/shard_map/stack | solution.py:19
  7.1 0.0 copy-start.3
  7.1 7.7 %all-to-all-start = ((bf16[32,32,1,64,128]{4,3,2,1,0:T(8,128)(2,1)}), bf16[32,32,1,64,128]{4,3,2,1,0:T(8,128)(2,1)}, u32[]{:S(2)}, u32[]{:S(2)}) async-start(bf16[32,32,1,64,128]{4,3,2,1,0:T(8,128)(2,1)} %stack.2), calls=%async_computation | async-start | bytes 33554432 | tf_op jit(solution)/shard_map/all_to_all | solution.py:19
  14.8 0.0 copy-done.3
  14.8 0.1 copy.10
  14.9 0.1 reshape_squeeze.6
  15.0 0.1 copy.9
  15.1 268.7 %all-to-all-done = bf16[32,32,1,64,128]{4,3,2,1,0:T(8,128)(2,1)} async-done(((bf16[32,32,1,64,128]{4,3,2,1,0:T(8,128)(2,1)}), bf16[32,32,1,64,128]{4,3,2,1,0:T(8,128)(2,1)}, u32[]{:S(2)}, u32[]{:S(2)}) %all-to-all-start) | async-done | bytes 16777248 | tf_op jit(solution)/shard_map/all_to_all | solution.py:19
  283.9 8.8 %gather_fusion = bf16[256,64,128]{2,1,0:T(8,128)(2,1)} fusion(bf16[1024,64,128]{2,1,0:T(8,128)(2,1)} %bitcast.2, s32[1024]{0:T(1024)S(1)} %pad_clamp_fusion), kind=kCustom, calls=%fused_computation | custom fusion | bytes 8389632 | tf_op jit(solution)/shard_map/jit(_take)/gather | solution.py:21
  292.7 0.0 copy-start.2
  292.7 0.0 copy-start.1
  292.7 6.6 %fusion.7 = f32[32,64,128]{2,1,0:T(8,128)S(1)} fusion(bf16[32,1,8,128,128]{4,3,2,1,0:T(8,128)(2,1)} %param.8, bf16[32,8,64,128]{3,2,1,0:T(8,128)(2,1)} %bitcast.73, pred[32,8]{1,0:T(8,128)(4,1)S(1)} %copy.9), kind=kOutput, calls=%fused_computation.10 | convolution fusion | flops 538968064 | bytes 13631744 | tf_op jit(solution)/shard_map/jkrm,jkmn->jrn/dot_general | solution.py:23
  299.3 0.0 copy-done
  299.3 0.0 copy-done.2
  299.3 0.4 convolution_add_fusion
  299.8 2.9 collective-permute-start
  302.7 4.1 %collective-permute-done = f32[64,128]{1,0:T(8,128)S(1)} collective-permute-done((f32[64,128]{1,0:T(8,128)S(1)}, f32[64,128]{1,0:T(8,128)S(1)}, u32[]{:S(2)}, u32[]{:S(2)}) %collective-permute-start) | collective-permute-done | bytes 32800 | tf_op jit(solution)/shard_map/ppermute | solution.py:10
  306.8 0.0 copy-done.1
  306.8 0.2 convolution_add_fusion.6
  306.9 1.9 collective-permute-start.1
  308.9 5.1 %collective-permute-done.1 = f32[64,128]{1,0:T(8,128)S(1)} collective-permute-done((f32[64,128]{1,0:T(8,128)S(1)}, f32[64,128]{1,0:T(8,128)S(1)}, u32[]{:S(2)}, u32[]{:S(2)}) %collective-permute-start.1) | collective-permute-done | bytes 32800 | tf_op jit(solution)/shard_map/ppermute | solution.py:10
  314.0 0.2 convolution_add_fusion.5
  314.1 1.9 collective-permute-start.2
  316.1 5.1 %collective-permute-done.2 = f32[64,128]{1,0:T(8,128)S(1)} collective-permute-done((f32[64,128]{1,0:T(8,128)S(1)}, f32[64,128]{1,0:T(8,128)S(1)}, u32[]{:S(2)}, u32[]{:S(2)}) %collective-permute-start.2) | collective-permute-done | bytes 32800 | tf_op jit(solution)/shard_map/ppermute | solution.py:10
  321.2 0.2 convolution_add_fusion.4
  321.3 1.9 collective-permute-start.3
  323.3 5.1 %collective-permute-done.3 = f32[64,128]{1,0:T(8,128)S(1)} collective-permute-done((f32[64,128]{1,0:T(8,128)S(1)}, f32[64,128]{1,0:T(8,128)S(1)}, u32[]{:S(2)}, u32[]{:S(2)}) %collective-permute-start.3) | collective-permute-done | bytes 32800 | tf_op jit(solution)/shard_map/ppermute | solution.py:10
  328.3 0.2 convolution_add_fusion.3
  328.5 1.9 collective-permute-start.4
  330.4 5.4 %collective-permute-done.4 = f32[64,128]{1,0:T(8,128)S(1)} collective-permute-done((f32[64,128]{1,0:T(8,128)S(1)}, f32[64,128]{1,0:T(8,128)S(1)}, u32[]{:S(2)}, u32[]{:S(2)}) %collective-permute-start.4) | collective-permute-done | bytes 32800 | tf_op jit(solution)/shard_map/ppermute | solution.py:10
  335.9 0.2 convolution_add_fusion.2
  336.0 1.9 collective-permute-start.5
  338.0 5.1 %collective-permute-done.5 = f32[64,128]{1,0:T(8,128)S(1)} collective-permute-done((f32[64,128]{1,0:T(8,128)S(1)}, f32[64,128]{1,0:T(8,128)S(1)}, u32[]{:S(2)}, u32[]{:S(2)}) %collective-permute-start.5) | collective-permute-done | bytes 32800 | tf_op jit(solution)/shard_map/ppermute | solution.py:10
  343.1 0.2 convolution_add_fusion.1
  343.2 1.9 collective-permute-start.6
  345.2 5.1 %collective-permute-done.6 = f32[64,128]{1,0:T(8,128)S(1)} collective-permute-done((f32[64,128]{1,0:T(8,128)S(1)}, f32[64,128]{1,0:T(8,128)S(1)}, u32[]{:S(2)}, u32[]{:S(2)}) %collective-permute-start.6) | collective-permute-done | bytes 32800 | tf_op jit(solution)/shard_map/ppermute | solution.py:10
  350.3 1.5 fusion.6
  (4 shorter events, 0.0 us)
Async XLA Ops:
  0.0 299.3 %copy-start = (bf16[32,1,128,128]{3,2,1,0:T(8,128)(2,1)S(1)}, bf16[32,1,128,128]{3,2,1,0:T(8,128)(2,1)}, u32[]{:S(2)}) copy-start(bf16[32,1,128,128]{3,2,1,0:T(8,128)(2,1)} %param.9) | copy-start | bytes 3145732
  7.1 7.7 %copy-start.3 = (s32[32,1,8]{0,2,1:T(8,128)S(1)}, s32[32,1,8]{0,2,1:T(8,128)}, u32[]{:S(2)}) copy-start(s32[32,1,8]{0,2,1:T(8,128)} %param.11) | copy-start | bytes 3076
  7.1 276.7 %all-to-all-start = ((bf16[32,32,1,64,128]{4,3,2,1,0:T(8,128)(2,1)}), bf16[32,32,1,64,128]{4,3,2,1,0:T(8,128)(2,1)}, u32[]{:S(2)}, u32[]{:S(2)}) async-start(bf16[32,32,1,64,128]{4,3,2,1,0:T(8,128)(2,1)} %stack.2), calls=%async_computation | async-start | bytes 33554432 | tf_op jit(solution)/shard_map/all_to_all | solution.py:19
  292.7 6.6 %copy-start.2 = (bf16[32,1,64,128]{3,2,1,0:T(8,128)(2,1)S(1)}, bf16[32,1,64,128]{3,2,1,0:T(8,128)(2,1)}, u32[]{:S(2)}) copy-start(bf16[32,1,64,128]{3,2,1,0:T(8,128)(2,1)} %param.7) | copy-start | bytes 1572868
  292.7 14.1 %copy-start.1 = (bf16[32,1,128,128]{3,2,1,0:T(8,128)(2,1)S(1)}, bf16[32,1,128,128]{3,2,1,0:T(8,128)(2,1)}, u32[]{:S(2)}) copy-start(bf16[32,1,128,128]{3,2,1,0:T(8,128)(2,1)} %param.10) | copy-start | bytes 3145732
  299.8 7.0 %collective-permute-start = (f32[64,128]{1,0:T(8,128)S(1)}, f32[64,128]{1,0:T(8,128)S(1)}, u32[]{:S(2)}, u32[]{:S(2)}) collective-permute-start(f32[64,128]{1,0:T(8,128)S(1)} %slice_bitcast_fusion), channel_id=1, source_target_pairs={{0,1},{1,2},{2,3},{3,4},{4,5},{5,6},{6,7},{8,9},{9,10},{10,11},{11... | collective-permute-start | bytes 98312 | tf_op jit(solution)/shard_map/ppermute | solution.py:10
  306.9 7.0 %collective-permute-start.1 = (f32[64,128]{1,0:T(8,128)S(1)}, f32[64,128]{1,0:T(8,128)S(1)}, u32[]{:S(2)}, u32[]{:S(2)}) collective-permute-start(f32[64,128]{1,0:T(8,128)S(1)} %convolution_add_fusion.6), channel_id=1, source_target_pairs={{0,1},{1,2},{2,3},{3,4},{4,5},{5,6},{6,7},{8,9},{9,10},{10,11},{11... | collective-permute-start | bytes 98312 | tf_op jit(solution)/shard_map/ppermute | solution.py:10
  314.1 7.0 %collective-permute-start.2 = (f32[64,128]{1,0:T(8,128)S(1)}, f32[64,128]{1,0:T(8,128)S(1)}, u32[]{:S(2)}, u32[]{:S(2)}) collective-permute-start(f32[64,128]{1,0:T(8,128)S(1)} %convolution_add_fusion.5), channel_id=1, source_target_pairs={{0,1},{1,2},{2,3},{3,4},{4,5},{5,6},{6,7},{8,9},{9,10},{10,11},{11... | collective-permute-start | bytes 98312 | tf_op jit(solution)/shard_map/ppermute | solution.py:10
  321.3 7.0 %collective-permute-start.3 = (f32[64,128]{1,0:T(8,128)S(1)}, f32[64,128]{1,0:T(8,128)S(1)}, u32[]{:S(2)}, u32[]{:S(2)}) collective-permute-start(f32[64,128]{1,0:T(8,128)S(1)} %convolution_add_fusion.4), channel_id=1, source_target_pairs={{0,1},{1,2},{2,3},{3,4},{4,5},{5,6},{6,7},{8,9},{9,10},{10,11},{11... | collective-permute-start | bytes 98312 | tf_op jit(solution)/shard_map/ppermute | solution.py:10
  328.5 7.4 %collective-permute-start.4 = (f32[64,128]{1,0:T(8,128)S(1)}, f32[64,128]{1,0:T(8,128)S(1)}, u32[]{:S(2)}, u32[]{:S(2)}) collective-permute-start(f32[64,128]{1,0:T(8,128)S(1)} %convolution_add_fusion.3), channel_id=1, source_target_pairs={{0,1},{1,2},{2,3},{3,4},{4,5},{5,6},{6,7},{8,9},{9,10},{10,11},{11... | collective-permute-start | bytes 98312 | tf_op jit(solution)/shard_map/ppermute | solution.py:10
  336.0 7.0 %collective-permute-start.5 = (f32[64,128]{1,0:T(8,128)S(1)}, f32[64,128]{1,0:T(8,128)S(1)}, u32[]{:S(2)}, u32[]{:S(2)}) collective-permute-start(f32[64,128]{1,0:T(8,128)S(1)} %convolution_add_fusion.2), channel_id=1, source_target_pairs={{0,1},{1,2},{2,3},{3,4},{4,5},{5,6},{6,7},{8,9},{9,10},{10,11},{11... | collective-permute-start | bytes 98312 | tf_op jit(solution)/shard_map/ppermute | solution.py:10
  343.2 7.0 %collective-permute-start.6 = (f32[64,128]{1,0:T(8,128)S(1)}, f32[64,128]{1,0:T(8,128)S(1)}, u32[]{:S(2)}, u32[]{:S(2)}) collective-permute-start(f32[64,128]{1,0:T(8,128)S(1)} %convolution_add_fusion.1), channel_id=1, source_target_pairs={{0,1},{1,2},{2,3},{3,4},{4,5},{5,6},{6,7},{8,9},{9,10},{10,11},{11... | collective-permute-start | bytes 98312 | tf_op jit(solution)/shard_map/ppermute | solution.py:10
